TPU v7x, 256 devices: a whole 4x4x8 slice. The times are simulated.
256 devices in a mesh: row: 8 (over z), col: 16 (over y, x), smp: 2 (over core).
Axes of the slice: x: 4, y: 4, z: 8, core: 2. Of those that a mesh axis runs over, the one named last changes fastest.
Arguments:
- state: float32 [8, 2048, 512], P('smp', ('row', 'col')), may hold values from -6 to 6
- noise: float32 [2, 8, 2048, 512], P(None, 'smp', ('row', 'col')), may hold values from -6 to 6
- pair: bfloat16 [2048, 2048, 128], P('row', 'col'), may hold values from -10 to 10
- contacts: int32 [16, 6], replicated, may hold values from -1 to 15, as said below
- norm_gain: float32 [512], replicated, may hold values from 0.1 to 1.9
- w_qkv: bfloat16 [512, 1536], replicated, may hold values from -0.25 to 0.25
- w_out: bfloat16 [512, 512], replicated, may hold values from -0.25 to 0.25
- w_bias: bfloat16 [128, 32], replicated, may hold values from -1.5 to 1.5
Outputs:
- denoised: float32 [8, 2048, 512], P('smp', ('row', 'col'))
Inputs may be any that keep to these rules, and one draw needn't show every extreme that they name: `contacts`: row q lists distinct blocks, q itself first, then nearby blocks more often than far ones; its first counts are blocks and the remaining slots hold -1; some row uses all 6 slots.
All inputs are finite; a program needn't handle non-finite values.
Results may differ from a plain program's by a relative error of at most 0.012.
Values may be sent and summed in bfloat16 or wider, within the bound.
A program may use at most 128 MiB of HBM per device.

v0:
```python
import jax
import jax.numpy as jnp
from jax import lax
from jax.sharding import PartitionSpec as P

STEPS = 2


def from_root(block, axis, owner):
    block = jnp.where(lax.axis_index(axis) == owner, block, jnp.zeros_like(block))
    return lax.psum(block, axis)


def body(state, noise, pair, contacts, norm_gain, w_qkv, w_out, w_bias):
    samples_dev, rows_dev, width = state.shape
    heads = w_bias.shape[1]
    head_dim = width // heads
    row_span, blk = (pair.shape[0], pair.shape[1])
    per_row = row_span // blk
    half = row_span // lax.axis_size("smp")
    own_rows = lax.dynamic_slice_in_dim(pair, lax.axis_index("smp") * half, half, 0)
    part_bias = jnp.einsum(
        "ijc,ch->hij", own_rows, w_bias, preferred_element_type=jnp.float32
    ).astype(jnp.bfloat16)
    bias = lax.all_gather(part_bias, "smp", axis=1, tiled=True).astype(jnp.float32)
    col_index = lax.axis_index("col")
    row_index = lax.axis_index("row")
    listed = lax.dynamic_slice_in_dim(contacts, row_index * per_row, per_row, 0)
    matched = jnp.any(listed == col_index, axis=1)
    allowed = jnp.repeat(matched, blk, total_repeat_length=row_span)
    busy = jnp.any(matched)
    x = state
    for step in range(STEPS):
        mean = jnp.mean(x, axis=-1, keepdims=True)
        var = jnp.mean((x - mean) ** 2, axis=-1, keepdims=True)
        normed = ((x - mean) * lax.rsqrt(var + 1e-05) * norm_gain).astype(jnp.bfloat16)
        qkv = jnp.dot(normed, w_qkv, preferred_element_type=jnp.float32).astype(jnp.bfloat16)
        block_rows = lax.all_gather(qkv, "col", axis=1, tiled=True)
        offset = col_index % per_row * blk
        mine = lax.dynamic_slice_in_dim(block_rows[..., width:], offset, blk, 1)
        keyval = from_root(mine, "row", col_index // per_row)
        queries = block_rows[..., :width].reshape(samples_dev, row_span, heads, head_dim)
        keys = keyval[..., :width].reshape(samples_dev, blk, heads, head_dim)
        values = keyval[..., width:].reshape(samples_dev, blk, heads, head_dim)

        def attend(unused):
            scores = (
                jnp.einsum("srhd,skhd->hsrk", queries, keys, preferred_element_type=jnp.float32)
                * 0.25
                + bias[:, None]
            )
            m_raw = jnp.max(scores, axis=-1)
            m_blk = jnp.where(allowed[None, None, :], m_raw, jnp.float32(-1e30))
            probs = jnp.where(
                allowed[None, None, :, None], jnp.exp(scores - m_raw[..., None]), jnp.float32(0.0)
            )
            totals = jnp.sum(probs, axis=-1)
            outputs = jnp.einsum(
                "hsrk,skhd->srhd",
                probs.astype(jnp.bfloat16),
                values,
                preferred_element_type=jnp.float32,
            )
            return (
                m_blk.transpose(1, 2, 0),
                totals.transpose(1, 2, 0),
                outputs.reshape(samples_dev, row_span, width),
            )

        def skipped(unused):
            return (
                jnp.full((samples_dev, row_span, heads), -1e30, jnp.float32),
                jnp.zeros((samples_dev, row_span, heads), jnp.float32),
                jnp.zeros((samples_dev, row_span, width), jnp.float32),
            )

        m_blk, totals, outputs = lax.cond(busy, attend, skipped, 0)
        top = lax.pmax(m_blk.astype(jnp.bfloat16), "col").astype(m_blk.dtype)
        weight = jnp.exp(m_blk - top)
        scaled = (
            outputs.reshape(samples_dev, row_span, heads, head_dim) * weight[..., None]
        ).reshape(samples_dev, row_span, width)
        summed, acc = (
            lax.psum_scatter(totals * weight, "col", scatter_dimension=1, tiled=True),
            lax.psum_scatter(scaled, "col", scatter_dimension=1, tiled=True),
        )
        attn = (acc.reshape(samples_dev, rows_dev, heads, head_dim) / summed[..., None]).reshape(
            samples_dev, rows_dev, width
        )
        attn = attn.astype(jnp.bfloat16)
        out = jnp.dot(attn, w_out, preferred_element_type=jnp.float32)
        x = x + out + 0.5 * 0.5**step * noise[step]
    return x


def solution(mesh):
    in_specs = (
        P("smp", ("row", "col"), None),
        P(None, "smp", ("row", "col"), None),
        P("row", "col", None),
        P(),
        P(),
        P(),
        P(),
        P(),
    )
    out_specs = P("smp", ("row", "col"), None)
    return jax.shard_map(body, mesh=mesh, in_specs=in_specs, out_specs=out_specs, check_vma=False)
```

profile of v0, /device:TPU:1, one launch (start us, length us, event | category | flops | bytes accessed | tf_op | source)
XLA Modules:
  0.0 770.3 jit_solution(14538606355737976069)
XLA Ops:
  10.8 4.8 fusion.23
  15.7 51.2 %all-gather.4.cloned.1.call-done = bf16[4,256,1536]{2,1,0:T(8,128)(2,1)} async-done(((bf16[4,16,1536]{2,1,0:T(8,128)(2,1)}), bf16[4,256,1536]{2,1,0:T(8,128)(2,1)}) %all-gather.4.cloned.1.call-update) | async-done | bytes 3145744 | tf_op jit(solution)/shard_map/all_gather | solution.py:38
  73.0 11.8 %all-gather.6.cloned.1.call-done = bf16[32,256,128]{2,0,1:T(8,128)(2,1)} async-done(((bf16[32,128,128]{2,0,1:T(8,128)(2,1)}), bf16[32,256,128]{2,0,1:T(8,128)(2,1)}) %all-gather.6.cloned.1.call-update) | async-done | bytes 2097168 | tf_op jit(solution)/shard_map/all_gather | solution.py:25
  84.8 4.1 convert_element_type.54
  88.9 70.4 %all-reduce.13.cloned.1.call-done = bf16[4,128,1024]{2,1,0:T(8,128)(2,1)} async-done(((bf16[4,128,1024]{2,1,0:T(8,128)(2,1)}), bf16[4,128,1024]{2,1,0:T(8,128)(2,1)}) %all-reduce.13.cloned.1.call-update) | async-done | bytes 1048592 | tf_op jit(solution)/shard_map/psum | solution.py:11
  159.4 29.7 %conditional.2 = (f32[4,256,512]{1,2,0:T(8,128)}, f32[4,256,32]{1,2,0:T(8,128)}, f32[4,256,32]{1,2,0:T(8,128)}) conditional(s32[]{:T(128)} %convert_element_type.49, () %tuple.25, (pred[256]{0:T(512)(128)(4,1)S(1)}, bf16[4,256,1536]{2,1,0:T(8,128)(2,1)}, bf16[4,128,1024]{2,1,0:T(8,128)(2,1)}, f32[32,256,128]{2,0,1:T(8,128)}) %tuple.26), branch_computations={%region_5.6_spmd, %region_6.9_spmd} | conditional | flops 306151424 | bytes 102367824 | solution.py:77
  159.4 5.3 copy.95
  167.1 4.6 copy.93
  173.1 5.4 fusion
  178.5 6.6 fusion.2
  190.7 93.2 %all-reduce.15.cloned.1.call-done = bf16[4,256,32]{1,2,0:T(8,128)(2,1)} async-done(((bf16[4,256,32]{1,2,0:T(8,128)(2,1)}), bf16[4,256,32]{1,2,0:T(8,128)(2,1)}) %all-reduce.15.cloned.1.call-update) | async-done | bytes 65552 | tf_op jit(solution)/shard_map/pmax | solution.py:78
  284.9 3.2 bitcast_multiply_fusion.1
  288.1 3.1 copy.98
  293.6 102.3 %all-reduce.23.cloned.1.call-done = (f32[4,256,32]{2,0,1:T(4,128)}, f32[4,256,512]{2,0,1:T(4,128)}) async-done(((f32[4,256,32]{2,0,1:T(4,128)}, f32[4,256,512]{2,0,1:T(4,128)}), (f32[4,256,32]{2,0,1:T(4,128)}, f32[4,256,512]{2,0,1:T(4,128)})) %all-reduce.23.cloned.1.call-update) | async-done | bytes 2228240
  401.9 52.4 %all-gather.8.cloned.1.call-done = bf16[4,256,1536]{2,1,0:T(8,128)(2,1)} async-done(((bf16[4,16,1536]{2,1,0:T(8,128)(2,1)}), bf16[4,256,1536]{2,1,0:T(8,128)(2,1)}) %all-gather.8.cloned.1.call-update) | async-done | bytes 3145744 | tf_op jit(solution)/shard_map/all_gather | solution.py:38
  457.3 71.1 %all-reduce.17.cloned.1.call-done = bf16[4,128,1024]{2,1,0:T(8,128)(2,1)} async-done(((bf16[4,128,1024]{2,1,0:T(8,128)(2,1)}), bf16[4,128,1024]{2,1,0:T(8,128)(2,1)}) %all-reduce.17.cloned.1.call-update) | async-done | bytes 1048592 | tf_op jit(solution)/shard_map/psum | solution.py:11
  528.4 25.1 %conditional.3 = (f32[4,256,512]{1,2,0:T(8,128)}, f32[4,256,32]{1,2,0:T(8,128)S(1)}, f32[4,256,32]{1,2,0:T(8,128)S(1)}) conditional(s32[]{:T(128)} %convert_element_type.49, () %tuple.27, (pred[256]{0:T(512)(128)(4,1)S(1)}, bf16[4,256,1536]{2,1,0:T(8,128)(2,1)}, bf16[4,128,1024]{2,1,0:T(8,128)(2,1)}, f32[32,256,128]{2,0,1:T(8,128)}) %tuple.28), branch_computations={%region_15.16_spmd, %region_16.19_spmd} | conditional | flops 306151424 | bytes 106037840 | solution.py:77
  528.4 5.4 copy.105
  534.5 4.6 copy.103
  540.5 4.5 fusion.8
  545.0 5.8 fusion.10
  554.2 93.3 %all-reduce.19.cloned.1.call-done = bf16[4,256,32]{1,2,0:T(8,128)(2,1)} async-done(((bf16[4,256,32]{1,2,0:T(8,128)(2,1)}), bf16[4,256,32]{1,2,0:T(8,128)(2,1)}) %all-reduce.19.cloned.1.call-update) | async-done | bytes 65552 | tf_op jit(solution)/shard_map/pmax | solution.py:78
  651.5 3.2 copy.108
  655.7 103.6 %all-reduce.21.cloned.1.call-done = (f32[4,256,32]{2,0,1:T(4,128)}, f32[4,256,512]{2,0,1:T(4,128)}) async-done(((f32[4,256,32]{2,0,1:T(4,128)}, f32[4,256,512]{2,0,1:T(4,128)}), (f32[4,256,32]{2,0,1:T(4,128)}, f32[4,256,512]{2,0,1:T(4,128)})) %all-reduce.21.cloned.1.call-update) | async-done | bytes 2228240
  (95 shorter events, 45.4 us)
Async XLA Ops:
  6.5 2.2 copy-start
  6.5 60.4 %all-gather.4.cloned.1.call-start = ((), (), s32[]{:S(2)}) async-start(), calls=%async_computation | async-start | bytes 3342336 | tf_op jit(solution)/shard_map/all_gather | solution.py:38
  10.8 74.0 %all-gather.6.cloned.1.call-start = ((), (), s32[]{:S(2)}) async-start(), calls=%async_computation.2 | async-start | bytes 3145728 | tf_op jit(solution)/shard_map/all_gather | solution.py:25
  15.6 54.2 %copy-start.9 = (s32[16,6]{0,1:T(8,128)S(1)}, s32[16,6]{0,1:T(8,128)}, u32[]{:S(2)}) copy-start(s32[16,6]{0,1:T(8,128)} %param.17) | copy-start | bytes 1156
  15.6 143.7 %all-reduce.13.cloned.1.call-start = ((), (), s32[]{:S(2)}) async-start(), calls=%async_computation.1 | async-start | bytes 2097152 | tf_op jit(solution)/shard_map/psum | solution.py:11
  66.9 1.6 slice-start
  69.7 214.2 %all-reduce.15.cloned.1.call-start = ((), (), s32[]{:S(2)}) async-start(), calls=%async_computation.3 | async-start | bytes 131072 | tf_op jit(solution)/shard_map/pmax | solution.py:78
  173.1 5.4 copy-start.2
  178.5 6.6 copy-start.6
  190.6 205.4 %all-reduce.23.cloned.1.call-start = ((), (), s32[]{:S(2)}) async-start(), calls=%async_computation.8 | async-start | bytes 5242880
  288.1 4.3 copy-start.10
  288.1 111.2 %copy-start.4 = (f32[4,16,512]{2,1,0:T(8,128)S(1)}, f32[4,16,512]{2,1,0:T(8,128)}, u32[]{:S(2)}) copy-start(f32[4,16,512]{2,1,0:T(8,128)} %param.14) | copy-start | bytes 393220
  288.1 111.2 %copy-start.5 = (bf16[512,512]{1,0:T(8,128)(2,1)S(1)}, bf16[512,512]{1,0:T(8,128)(2,1)}, u32[]{:S(2)}) copy-start(bf16[512,512]{1,0:T(8,128)(2,1)} %param.20) | copy-start | bytes 1572868
  291.2 109.5 %copy-start.8 = (f32[512]{0:T(512)S(1)}, f32[512]{0:T(512)}, u32[]{:S(2)}) copy-start(f32[512]{0:T(512)} %param.18) | copy-start | bytes 6148
  292.3 162.0 %all-gather.8.cloned.1.call-start = ((), (), s32[]{:S(2)}) async-start(), calls=%async_computation.4 | async-start | bytes 3342336 | tf_op jit(solution)/shard_map/all_gather | solution.py:38
  401.9 126.5 %all-reduce.17.cloned.1.call-start = ((), (), s32[]{:S(2)}) async-start(), calls=%async_computation.5 | async-start | bytes 2097152 | tf_op jit(solution)/shard_map/psum | solution.py:11
  454.4 1.6 slice-start.1
  457.2 190.3 %all-reduce.19.cloned.1.call-start = ((), (), s32[]{:S(2)}) async-start(), calls=%async_computation.6 | async-start | bytes 131072 | tf_op jit(solution)/shard_map/pmax | solution.py:78
  528.4 5.4 copy-start.7
  540.4 4.5 copy-start.3
  554.2 205.2 %all-reduce.21.cloned.1.call-start = ((), (), s32[]{:S(2)}) async-start(), calls=%async_computation.7 | async-start | bytes 5242880
  651.5 112.3 %copy-start.1 = (bf16[512,1536]{1,0:T(8,128)(2,1)S(1)}, bf16[512,1536]{1,0:T(8,128)(2,1)}, u32[]{:S(2)}) copy-start(bf16[512,1536]{1,0:T(8,128)(2,1)} %param.19) | copy-start | bytes 4718596
Sparse Core Ops, SparseCore 0:
  10.9 55.9 all-gather.3
  68.7 16.0 all-gather.5
  87.2 72.1 all-reduce.12
  190.7 93.1 all-reduce.14
  292.5 103.4 all-reduce.22
  402.0 52.3 all-gather.7
  457.3 71.0 all-reduce.16
  554.3 93.1 all-reduce.18
  655.8 103.4 all-reduce.20
where the time goes:
time: 771 us; the launch traced here: 770 us
  waiting for transfers between devices  650 us (84%)
  local copies, waits for them, and re-layouts  45.9 us (6%)
  other arithmetic  33.8 us (4%)
  matrix products  26 us (3%)
  between operations  14.7 us (2%)
    unnamed x11, waiting for transfers between devices  206 us
    pmax x2, waiting for transfers between devices, body(): top = lax.pmax(m_blk.astype(jnp.bfloat16), 'col').astype(m_blk.dtype)  187 us
    psum x2, waiting for transfers between devices, from_root(): return lax.psum(block, axis)  142 us
    all_gather x2, waiting for transfers between devices, body(): block_rows = lax.all_gather(qkv, 'col', axis=1, tiled=True)  104 us
    another operation x6, local copies, waits for them, and re-layouts  22.2 us
  transfers between devices with their start and end apart: 9, of which 9 were waited for; matrix products, arithmetic and copies ran while one was open for 2% of the time, Pallas kernels for 0%

commit v1 on v0

--- a/solution.py
+++ b/solution.py
@@ -8,7 +8,11 @@
 
 def from_root(block, axis, owner):
     block = jnp.where(lax.axis_index(axis) == owner, block, jnp.zeros_like(block))
-    return lax.psum(block, axis)
+
+    def _cover_tokens(local_x):
+        return lax.all_gather(local_x, axis_name=axis).sum(axis=0)
+
+    return _cover_tokens(block)
 
 
 def body(state, noise, pair, contacts, norm_gain, w_qkv, w_out, w_bias):

time: 771 us -> 820 us (1.064)
  waiting for transfers between devices: 650 us -> 685 us
  other arithmetic: 33.8 us -> 45.2 us
    all_gather x0 -> x2, waiting for transfers between devices: none -> 186 us  [_cover_tokens(): return lax.all_gather(local_x, axis_name=axis).sum(axis=0)]
    psum x2 -> x0, waiting for transfers between devices: 142 us -> none  [from_root(): return lax.psum(block, axis)]
    reduce_sum x0 -> x2, other arithmetic: none -> 11.2 us  [_cover_tokens(): return lax.all_gather(local_x, axis_name=axis).sum(axis=0)]
where the time goes in v1:
time: 820 us; the launch traced here: 819 us
  waiting for transfers between devices  685 us (84%)
  local copies, waits for them, and re-layouts  47.4 us (6%)
  other arithmetic  45.2 us (6%)
  matrix products  26 us (3%)
  between operations  14.7 us (2%)
    unnamed x11, waiting for transfers between devices  206 us
    all_gather x2, waiting for transfers between devices, _cover_tokens(): return lax.all_gather(local_x, axis_name=axis).sum(axis=0)  186 us
    pmax x2, waiting for transfers between devices, body(): top = lax.pmax(m_blk.astype(jnp.bfloat16), 'col').astype(m_blk.dtype)  178 us
    all_gather x2, waiting for transfers between devices, body(): block_rows = lax.all_gather(qkv, 'col', axis=1, tiled=True)  104 us
    another operation x6, local copies, waits for them, and re-layouts  21.8 us
  transfers between devices with their start and end apart: 9, of which 9 were waited for; matrix products, arithmetic and copies ran while one was open for 2% of the time, Pallas kernels for 0%

profile of v1, /device:TPU:1, one launch (start us, length us, event | category | flops | bytes accessed | tf_op | source)
XLA Modules:
  0.0 819.2 jit_solution(8088591402080817758)
XLA Ops:
  10.8 4.8 fusion.23
  15.7 51.2 %all-gather.8.cloned.1.call-done = bf16[4,256,1536]{2,1,0:T(8,128)(2,1)} async-done(((bf16[4,16,1536]{2,1,0:T(8,128)(2,1)}), bf16[4,256,1536]{2,1,0:T(8,128)(2,1)}) %all-gather.8.cloned.1.call-update) | async-done | bytes 3145744 | tf_op jit(solution)/shard_map/all_gather | solution.py:42
  73.1 11.7 %all-gather.10.cloned.1.call-done = bf16[32,256,128]{2,0,1:T(8,128)(2,1)} async-done(((bf16[32,128,128]{2,0,1:T(8,128)(2,1)}), bf16[32,256,128]{2,0,1:T(8,128)(2,1)}) %all-gather.10.cloned.1.call-update) | async-done | bytes 2097168 | tf_op jit(solution)/shard_map/all_gather | solution.py:29
  84.8 4.1 convert_element_type.58
  88.9 92.2 %all-gather.14.cloned.1.call-done = bf16[32,128,1024]{2,1,0:T(8,128)(2,1)} async-done(((bf16[4,128,1024]{2,1,0:T(8,128)(2,1)}), bf16[32,128,1024]{2,1,0:T(8,128)(2,1)}) %all-gather.14.cloned.1.call-update) | async-done | bytes 8388624 | tf_op jit(solution)/shard_map/all_gather | solution.py:13
  181.1 5.6 reduce_sum.80
  186.7 30.6 %conditional.2 = (f32[4,256,512]{1,2,0:T(8,128)}, f32[4,256,32]{1,2,0:T(8,128)}, f32[4,256,32]{1,2,0:T(8,128)}) conditional(s32[]{:T(128)} %convert_element_type.53, () %tuple.25, (pred[256]{0:T(512)(128)(4,1)S(1)}, bf16[4,256,1536]{2,1,0:T(8,128)(2,1)}, bf16[4,128,1024]{2,1,0:T(8,128)(2,1)S(1)}, f32[32,256,128]{2,0,1:T(8,128)}) %tuple.26), branch_computations={%region_5.6_spmd, %region_6.9_spmd} | conditional | flops 306151424 | bytes 102367824 | solution.py:81
  186.8 5.3 copy.91
  195.4 4.6 copy.89
  201.3 5.4 fusion
  206.8 6.6 fusion.2
  218.9 89.2 %all-reduce.11.cloned.1.call-done = bf16[4,256,32]{1,2,0:T(8,128)(2,1)} async-done(((bf16[4,256,32]{1,2,0:T(8,128)(2,1)}), bf16[4,256,32]{1,2,0:T(8,128)(2,1)}) %all-reduce.11.cloned.1.call-update) | async-done | bytes 65552 | tf_op jit(solution)/shard_map/pmax | solution.py:82
  309.1 3.2 bitcast_multiply_fusion.1
  317.9 102.2 %all-reduce.17.cloned.1.call-done = (f32[4,256,32]{2,0,1:T(4,128)}, f32[4,256,512]{2,0,1:T(4,128)}) async-done(((f32[4,256,32]{2,0,1:T(4,128)}, f32[4,256,512]{2,0,1:T(4,128)}), (f32[4,256,32]{2,0,1:T(4,128)}, f32[4,256,512]{2,0,1:T(4,128)})) %all-reduce.17.cloned.1.call-update) | async-done | bytes 2228240
  426.1 52.4 %all-gather.12.cloned.1.call-done = bf16[4,256,1536]{2,1,0:T(8,128)(2,1)} async-done(((bf16[4,16,1536]{2,1,0:T(8,128)(2,1)}), bf16[4,256,1536]{2,1,0:T(8,128)(2,1)}) %all-gather.12.cloned.1.call-update) | async-done | bytes 3145744 | tf_op jit(solution)/shard_map/all_gather | solution.py:42
  481.4 93.5 %all-gather.16.cloned.1.call-done = bf16[32,128,1024]{2,1,0:T(8,128)(2,1)} async-done(((bf16[4,128,1024]{2,1,0:T(8,128)(2,1)}), bf16[32,128,1024]{2,1,0:T(8,128)(2,1)}) %all-gather.16.cloned.1.call-update) | async-done | bytes 8388624 | tf_op jit(solution)/shard_map/all_gather | solution.py:13
  574.8 5.6 reduce_sum.83
  580.5 25.9 %conditional.3 = (f32[4,256,512]{1,2,0:T(8,128)}, f32[4,256,32]{1,2,0:T(8,128)S(1)}, f32[4,256,32]{1,2,0:T(8,128)S(1)}) conditional(s32[]{:T(128)} %convert_element_type.53, () %tuple.27, (pred[256]{0:T(512)(128)(4,1)S(1)}, bf16[4,256,1536]{2,1,0:T(8,128)(2,1)}, bf16[4,128,1024]{2,1,0:T(8,128)(2,1)S(1)}, f32[32,256,128]{2,0,1:T(8,128)}) %tuple.28), branch_computations={%region_15.16_spmd, %region_16.19_spmd} | conditional | flops 306151424 | bytes 103940688 | solution.py:81
  580.5 5.3 copy.101
  587.3 4.7 copy.99
  593.3 4.5 fusion.8
  597.9 5.8 fusion.10
  607.1 89.2 %all-reduce.13.cloned.1.call-done = bf16[4,256,32]{1,2,0:T(8,128)(2,1)} async-done(((bf16[4,256,32]{1,2,0:T(8,128)(2,1)}), bf16[4,256,32]{1,2,0:T(8,128)(2,1)}) %all-reduce.13.cloned.1.call-update) | async-done | bytes 65552 | tf_op jit(solution)/shard_map/pmax | solution.py:82
  704.6 103.6 %all-reduce.15.cloned.1.call-done = (f32[4,256,32]{2,0,1:T(4,128)}, f32[4,256,512]{2,0,1:T(4,128)}) async-done(((f32[4,256,32]{2,0,1:T(4,128)}, f32[4,256,512]{2,0,1:T(4,128)}), (f32[4,256,32]{2,0,1:T(4,128)}, f32[4,256,512]{2,0,1:T(4,128)})) %all-reduce.15.cloned.1.call-update) | async-done | bytes 2228240
  (99 shorter events, 53.6 us)
Async XLA Ops:
  6.5 2.2 copy-start
  6.5 60.4 %all-gather.8.cloned.1.call-start = ((), (), s32[]{:S(2)}) async-start(), calls=%async_computation | async-start | bytes 3342336 | tf_op jit(solution)/shard_map/all_gather | solution.py:42
  10.8 74.0 %all-gather.10.cloned.1.call-start = ((), (), s32[]{:S(2)}) async-start(), calls=%async_computation.1 | async-start | bytes 3145728 | tf_op jit(solution)/shard_map/all_gather | solution.py:29
  15.6 54.2 %copy-start.10 = (s32[16,6]{0,1:T(8,128)S(1)}, s32[16,6]{0,1:T(8,128)}, u32[]{:S(2)}) copy-start(s32[16,6]{0,1:T(8,128)} %param.17) | copy-start | bytes 1156
  15.7 165.4 %all-gather.14.cloned.1.call-start = ((), (), s32[]{:S(2)}) async-start(), calls=%async_computation.5 | async-start | bytes 9437184 | tf_op jit(solution)/shard_map/all_gather | solution.py:13
  66.9 1.6 slice-start
  69.7 238.4 %all-reduce.11.cloned.1.call-start = ((), (), s32[]{:S(2)}) async-start(), calls=%async_computation.2 | async-start | bytes 131072 | tf_op jit(solution)/shard_map/pmax | solution.py:82
  201.3 5.4 copy-start.2
  206.8 6.6 copy-start.7
  218.9 201.3 %all-reduce.17.cloned.1.call-start = ((), (), s32[]{:S(2)}) async-start(), calls=%async_computation.8 | async-start | bytes 5242880
  312.3 4.4 copy-start.11
  312.3 111.1 %copy-start.4 = (f32[4,16,512]{2,1,0:T(8,128)S(1)}, f32[4,16,512]{2,1,0:T(8,128)}, u32[]{:S(2)}) copy-start(f32[4,16,512]{2,1,0:T(8,128)} %param.14) | copy-start | bytes 393220
  312.3 111.1 %copy-start.5 = (bf16[512,512]{1,0:T(8,128)(2,1)S(1)}, bf16[512,512]{1,0:T(8,128)(2,1)}, u32[]{:S(2)}) copy-start(bf16[512,512]{1,0:T(8,128)(2,1)} %param.20) | copy-start | bytes 1572868
  315.4 109.5 %copy-start.9 = (f32[512]{0:T(512)S(1)}, f32[512]{0:T(512)}, u32[]{:S(2)}) copy-start(f32[512]{0:T(512)} %param.18) | copy-start | bytes 6148
  316.5 162.1 %all-gather.12.cloned.1.call-start = ((), (), s32[]{:S(2)}) async-start(), calls=%async_computation.3 | async-start | bytes 3342336 | tf_op jit(solution)/shard_map/all_gather | solution.py:42
  426.0 148.8 %all-gather.16.cloned.1.call-start = ((), (), s32[]{:S(2)}) async-start(), calls=%async_computation.6 | async-start | bytes 9437184 | tf_op jit(solution)/shard_map/all_gather | solution.py:13
  478.5 1.6 slice-start.1
  481.3 215.0 %all-reduce.13.cloned.1.call-start = ((), (), s32[]{:S(2)}) async-start(), calls=%async_computation.4 | async-start | bytes 131072 | tf_op jit(solution)/shard_map/pmax | solution.py:82
  587.3 6.0 copy-start.6
  593.3 4.6 copy-start.3
  606.4 90.0 %copy-start.8 = (f32[4,256,32]{1,2,0:T(8,128)}, f32[4,256,32]{1,2,0:T(8,128)S(1)}, u32[]{:S(2)}) copy-start(f32[4,256,32]{1,2,0:T(8,128)S(1)} %get-tuple-element.110) | copy-start | bytes 393220
  607.1 201.2 %all-reduce.15.cloned.1.call-start = ((), (), s32[]{:S(2)}) async-start(), calls=%async_computation.7 | async-start | bytes 5242880
  700.4 112.3 %copy-start.1 = (bf16[512,1536]{1,0:T(8,128)(2,1)S(1)}, bf16[512,1536]{1,0:T(8,128)(2,1)}, u32[]{:S(2)}) copy-start(bf16[512,1536]{1,0:T(8,128)(2,1)} %param.19) | copy-start | bytes 4718596
Sparse Core Ops, SparseCore 0:
  10.9 55.9 all-gather.7
  68.7 16.0 all-gather.9
  86.6 94.4 all-gather.13
  219.0 89.0 all-reduce.10
  316.6 103.5 all-reduce.16
  426.2 52.3 all-gather.11
  481.5 93.3 all-gather.15
  607.2 89.1 all-reduce.12
  704.8 103.4 all-reduce.14
